TPU v7x, 256 devices: a whole 4x4x8 slice. The times are simulated.
256 devices in a mesh: dp: 32 (over z, x_hi, core), tensor: 8 (over x_lo, y).
Axes of the slice: x: 4 (x_hi: 2, x_lo: 2; x = x_hi * 2 + x_lo), y: 4, z: 8, core: 2. Of those that a mesh axis runs over, the one named last changes fastest.
Arguments:
- hidden: bfloat16 [16384, 14336], P('dp', 'tensor'), may hold values from -76 to 76
- base_weight: bfloat16 [14336, 4096], P('tensor', 'dp'), may hold values from -0.046875 to 0.046875
- adapter_in: bfloat16 [256, 14336], P(None, 'tensor'), may hold values from -0.046875 to 0.046875
- adapter_out: bfloat16 [256, 4096], P(None, 'tensor'), may hold values from -0.375 to 0.375
- cotangent: bfloat16 [16384, 4096], P('dp', 'tensor'), may hold values from -0.046875 to 0.046875
Outputs:
- output: bfloat16 [16384, 4096], P('dp', 'tensor')
- grad_in: float32 [256, 14336], P('dp', 'tensor')
- grad_out: float32 [256, 4096], P('dp', 'tensor')
All inputs are finite; a program needn't handle non-finite values.
Results may differ from a plain program's by a relative error of at most 0.0031.
Values may be sent and summed in bfloat16 or wider, within the bound.
A program may use at most 128 MiB of HBM per device.

v0:
```python
import jax
import jax.numpy as jnp
from jax import lax
from jax.sharding import PartitionSpec as P

adapter_scale = 4.0
exp_rate = 0.25
tiny_eps = 1e-06


def inverse_sinh(value):
    return jnp.log(value + jnp.sqrt(1.0 + value * value))


def shards(hidden, base_weight, adapter_in, adapter_out, cotangent):
    feature_count = hidden.shape[1] * lax.axis_size("tensor")
    contract_last = (((1,), (1,)), ((), ()))
    contract_first = (((0,), (0,)), ((), ()))
    square_part = jnp.sum(jnp.square(hidden.astype(jnp.float32)), axis=1)
    rank_part = lax.dot_general(
        hidden, adapter_in, contract_last, preferred_element_type=jnp.float32
    )
    square_sum, lorentz_raw = lax.psum((square_part, rank_part), "tensor")
    level = jnp.sqrt(square_sum / feature_count + tiny_eps)
    radius = exp_rate * level
    lift_factor = jnp.sinh(radius) / radius
    lorentz = lift_factor[:, None] * lorentz_raw
    norm_value = jnp.sqrt(jnp.sum(lorentz * lorentz, axis=1) + tiny_eps)
    phi_value = inverse_sinh(norm_value) / norm_value
    tangent = (phi_value[:, None] * lorentz).astype(jnp.bfloat16)
    partial_cols = jnp.dot(
        hidden,
        lax.all_gather(base_weight, "dp", axis=1, tiled=True),
        preferred_element_type=jnp.float32,
    )
    base_sum = lax.psum_scatter(partial_cols, "tensor", scatter_dimension=1, tiled=True)
    adapter_term = jnp.dot(tangent, adapter_out, preferred_element_type=jnp.float32)
    output = (base_sum + adapter_scale * adapter_term).astype(jnp.bfloat16)
    out_part = adapter_scale * lax.dot_general(
        tangent, cotangent, contract_first, preferred_element_type=jnp.float32
    )
    cotan_later = adapter_scale * lax.dot_general(
        cotangent, adapter_out, contract_last, preferred_element_type=jnp.float32
    )
    tangent_grad = lax.psum(cotan_later, "tensor")
    inner_value = jnp.sum(lorentz * tangent_grad, axis=1)
    coefficient = (1.0 / jnp.sqrt(1.0 + norm_value * norm_value) - phi_value) / (
        norm_value * norm_value
    )
    lorentz_grad = (
        phi_value[:, None] * tangent_grad + (coefficient * inner_value)[:, None] * lorentz
    )
    raw_grad = (lift_factor[:, None] * lorentz_grad).astype(jnp.bfloat16)
    in_part = lax.dot_general(raw_grad, hidden, contract_first, preferred_element_type=jnp.float32)
    grad_in, grad_out = (
        lax.psum_scatter(in_part, "dp", scatter_dimension=0, tiled=True),
        lax.psum_scatter(out_part, "dp", scatter_dimension=0, tiled=True),
    )
    return (output, grad_in, grad_out)


def solution(mesh):
    return jax.shard_map(
        shards,
        mesh=mesh,
        in_specs=(
            P("dp", "tensor"),
            P("tensor", "dp"),
            P(None, "tensor"),
            P(None, "tensor"),
            P("dp", "tensor"),
        ),
        out_specs=(P("dp", "tensor"), P("dp", "tensor"), P("dp", "tensor")),
        check_vma=False,
    )
```

profile of v0, /device:TPU:8, one launch (start us, length us, event | category | flops | bytes accessed | tf_op | source)
XLA Modules:
  0.0 506.5 jit_solution(1643194782338314883)
XLA Ops:
  8.0 0.0 copy-start
  8.0 0.0 all-gather.2.cloned.1.call-start
  8.1 0.7 all-gather.2.cloned.1.call-update
  8.7 0.0 all-reduce.3.cloned.1.call-start
  8.8 2.2 convolution_multiply_fusion.2
  11.0 0.0 copy-done
  11.0 0.0 copy-start.2
  11.0 3.1 fusion.12
  14.1 0.0 all-reduce.3.cloned.1.call-update
  14.2 0.0 reduce-scatter.4.cloned.1.call-start
  14.2 141.3 %all-gather.2.cloned.1.call-done = bf16[1792,4096]{1,0:T(8,128)(2,1)} async-done(((bf16[1792,128]{1,0:T(8,128)(2,1)}), bf16[1792,4096]{1,0:T(8,128)(2,1)}) %all-gather.2.cloned.1.call-update) | async-done | bytes 14680080 | tf_op jit(solution)/shard_map/all_gather | solution.py:33
  155.5 0.0 copy-done.2
  155.5 13.0 %fusion.11 = f32[512,4096]{1,0:T(8,128)} fusion(bf16[512,1792]{1,0:T(8,128)(2,1)S(1)} %copy-done.2, bf16[1792,4096]{1,0:T(8,128)(2,1)} %all-gather.2.cloned.1.call-done), kind=kOutput, calls=%fused_computation.25 | convolution fusion | flops 7516192768 | bytes 24903680 | tf_op jit(solution)/shard_map/dot_general | solution.py:31
  168.5 0.0 reduce-scatter.4.cloned.1.call-update
  168.5 0.0 reduce-scatter.8.cloned.1.call-start
  168.6 0.4 multiply_reduce_fusion
  169.0 16.6 %psum.21 = f32[512]{0:T(512)S(1)} all-reduce(f32[512]{0:T(512)S(1)} %multiply_reduce_fusion), channel_id=1, replica_groups=mesh['dp'=32,'tensor'=8] {'tensor'}, use_global_device_ids=true, to_apply=%region_2.0 | all-reduce | flops 512 | bytes 4096 | tf_op jit(solution)/shard_map/psum | solution.py:23
  185.7 0.0 all-reduce.3.cloned.1.call-done
  185.7 0.0 copy-start.1
  185.7 1.6 multiply_reduce_fusion.1
  187.3 2.6 convolution_multiply_fusion.1
  189.9 0.0 reduce-scatter.8.cloned.1.call-update
  190.0 0.0 reduce-scatter.6.cloned.1.call-start
  190.0 0.0 copy-done.1
  190.0 3.1 fusion.2
  193.2 0.0 copy-start.3
  193.2 0.0 reduce-scatter.6.cloned.1.call-update
  193.2 64.9 %reduce-scatter.4.cloned.1.call-done = f32[512,512]{1,0:T(8,128)} async-done(((f32[512,4096]{1,0:T(8,128)}), f32[512,512]{1,0:T(8,128)}) %reduce-scatter.4.cloned.1.call-update) | async-done | bytes 1048592 | tf_op jit(solution)/shard_map/reduce_scatter | solution.py:36
  258.1 0.0 copy-done.3
  258.1 2.4 fusion.1
  260.5 116.9 %reduce-scatter.8.cloned.1.call-done = f32[8,512]{1,0:T(8,128)} async-done(((f32[256,512]{1,0:T(8,128)}), f32[8,512]{1,0:T(8,128)}) %reduce-scatter.8.cloned.1.call-update) | async-done | bytes 16400 | tf_op jit(solution)/shard_map/reduce_scatter | solution.py:57
  377.3 121.6 %reduce-scatter.6.cloned.1.call-done = f32[8,1792]{1,0:T(8,128)} async-done(((f32[256,1792]{1,0:T(8,128)}), f32[8,1792]{1,0:T(8,128)}) %reduce-scatter.6.cloned.1.call-update) | async-done | bytes 57360 | tf_op jit(solution)/shard_map/reduce_scatter | solution.py:56
  (2 shorter events, 0.1 us)
Async XLA Ops:
  8.0 3.0 copy-start
  8.0 147.5 %all-gather.2.cloned.1.call-start = ((), (), s32[]{:S(2)}) async-start(), calls=%async_computation.3 | async-start | bytes 15138816 | tf_op jit(solution)/shard_map/all_gather | solution.py:33
  8.7 176.9 %all-reduce.3.cloned.1.call-start = ((), (), s32[]{:S(2)}) async-start(), calls=%async_computation.7 | async-start | bytes 2097152 | tf_op jit(solution)/shard_map/psum | solution.py:23
  11.0 144.5 %copy-start.2 = (bf16[512,1792]{1,0:T(8,128)(2,1)S(1)}, bf16[512,1792]{1,0:T(8,128)(2,1)}, u32[]{:S(2)}) copy-start(bf16[512,1792]{1,0:T(8,128)(2,1)} %param.5) | copy-start | bytes 5505028
  14.2 243.9 %reduce-scatter.4.cloned.1.call-start = ((), (), s32[]{:S(2)}) async-start(), calls=%async_computation.4 | async-start | bytes 9437184 | tf_op jit(solution)/shard_map/reduce_scatter | solution.py:36
  168.5 208.8 %reduce-scatter.8.cloned.1.call-start = ((), (), s32[]{:S(2)}) async-start(), calls=%async_computation.6 | async-start | bytes 540672 | tf_op jit(solution)/shard_map/reduce_scatter | solution.py:57
  185.7 4.3 copy-start.1
  190.0 308.9 %reduce-scatter.6.cloned.1.call-start = ((), (), s32[]{:S(2)}) async-start(), calls=%async_computation.5 | async-start | bytes 1892352 | tf_op jit(solution)/shard_map/reduce_scatter | solution.py:56
  193.2 64.9 %copy-start.3 = (bf16[256,512]{1,0:T(8,128)(2,1)S(1)}, bf16[256,512]{1,0:T(8,128)(2,1)}, u32[]{:S(2)}) copy-start(bf16[256,512]{1,0:T(8,128)(2,1)} %param.8) | copy-start | bytes 786436
Sparse Core Ops, SparseCore 0:
  11.4 144.0 all-gather.1
Sparse Core Ops, SparseCore 1:
  14.2 125.5 all-reduce.2
  168.6 89.4 reduce-scatter.3
  262.6 114.7 reduce-scatter.7
  382.6 116.2 reduce-scatter.5
where the time goes:
time: 507 us
  waiting for transfers between devices  445 us (88%)
  matrix products  26.5 us (5%)
  blocking collectives  16.6 us (3%)
  between operations  15.7 us (3%)
    all_gather x1, waiting for transfers between devices, shards(): lax.all_gather(base_weight, 'dp', axis=1, tiled=True)  141 us
    reduce_scatter x1, waiting for transfers between devices, shards(): lax.psum_scatter(in_part, 'dp', scatter_dimension=0, tiled=True)  122 us
    reduce_scatter x1, waiting for transfers between devices, shards(): lax.psum_scatter(out_part, 'dp', scatter_dimension=0, tiled=True)  117 us
    reduce_scatter x1, waiting for transfers between devices, shards(): lax.psum_scatter(partial_cols, 'tensor', scatter_dimension=1, tiled=True)  64.9 us
    psum x1, blocking collectives, shards(): square_sum, lorentz_raw = lax.psum((square_part, rank_part), 'tensor')  16.6 us
    dot_general x1, matrix products, shards(): jnp.dot(hidden, lax.all_gather(base_weight, 'dp', axis=1, tiled=True), pr...  13 us
  transfers between devices with their start and end apart: 5, of which 4 were waited for; matrix products, arithmetic and copies ran while one was open for 6% of the time, Pallas kernels for 0%

commit v1 on v0

--- a/solution.py
+++ b/solution.py
@@ -30,7 +30,9 @@
     tangent = (phi_value[:, None] * lorentz).astype(jnp.bfloat16)
     partial_cols = jnp.dot(
         hidden,
-        lax.all_gather(base_weight, "dp", axis=1, tiled=True),
+        jnp.concatenate(
+            lax.all_to_all(jnp.stack([base_weight] * lax.axis_size("dp")), "dp", 0, 0), axis=1
+        ),
         preferred_element_type=jnp.float32,
     )
     base_sum = lax.psum_scatter(partial_cols, "tensor", scatter_dimension=1, tiled=True)

time: 507 us -> 700 us (1.38)
  waiting for transfers between devices: 445 us -> 623 us
  starting transfers between devices: 0.21 us -> 11.9 us
  local copies, waits for them, and re-layouts: 0.02 us -> 8.19 us
    all_to_all x0 -> x1, waiting for transfers between devices: none -> 312 us  [shards(): lax.all_to_all(jnp.stack([base_weight] * lax.axis_size('dp')), 'dp', 0, 0)]
    all_gather x1 -> x0, waiting for transfers between devices: 141 us -> none  [shards(): lax.all_gather(base_weight, 'dp', axis=1, tiled=True)]
    all_to_all x0 -> x1, starting transfers between devices: none -> 11.7 us  [shards(): lax.all_to_all(jnp.stack([base_weight] * lax.axis_size('dp')), 'dp', 0, 0)]
    reduce_scatter x1, waiting for transfers between devices: 64.9 us -> 73.3 us  [shards(): lax.psum_scatter(partial_cols, 'tensor', scatter_dimension=1, tiled=True)]
  transfers between devices with their start and end apart: 5 -> 5, of which waited for: 4 -> 4; matrix products, arithmetic and copies ran while one was open for 6% -> 4% of each run, Pallas kernels for 0% -> 0%
where the time goes in v1:
time: 700 us
  waiting for transfers between devices  623 us (89%)
  matrix products  23.8 us (3%)
  blocking collectives  16.4 us (2%)
  between operations  13.8 us (2%)
  starting transfers between devices  11.9 us (2%)
  local copies, waits for them, and re-layouts  8.19 us (1%)
    all_to_all x1, waiting for transfers between devices, shards(): lax.all_to_all(jnp.stack([base_weight] * lax.axis_size('dp')), 'dp', 0, 0)  312 us
    reduce_scatter x1, waiting for transfers between devices, shards(): lax.psum_scatter(in_part, 'dp', scatter_dimension=0, tiled=True)  121 us
    reduce_scatter x1, waiting for transfers between devices, shards(): lax.psum_scatter(out_part, 'dp', scatter_dimension=0, tiled=True)  117 us
    reduce_scatter x1, waiting for transfers between devices, shards(): lax.psum_scatter(partial_cols, 'tensor', scatter_dimension=1, tiled=True)  73.3 us
    psum x1, blocking collectives, shards(): square_sum, lorentz_raw = lax.psum((square_part, rank_part), 'tensor')  16.4 us
  transfers between devices with their start and end apart: 5, of which 4 were waited for; matrix products, arithmetic and copies ran while one was open for 4% of the time, Pallas kernels for 0%

profile of v1, /device:TPU:8, one launch (start us, length us, event | category | flops | bytes accessed | tf_op | source)
XLA Modules:
  0.0 699.5 jit_solution(1424321645614266320)
XLA Ops:
  7.2 0.0 copy-start
  7.2 1.3 copy.8
  8.5 6.9 stack.2
  15.4 11.7 %all-to-all-start = ((bf16[32,1792,128]{1,2,0:T(8,128)(2,1)}), bf16[32,1792,128]{1,2,0:T(8,128)(2,1)}, u32[]{:S(2)}, u32[]{:S(2)}) async-start(bf16[32,1792,128]{1,2,0:T(8,128)(2,1)} %stack.2), calls=%async_computation | async-start | bytes 29360128 | tf_op jit(solution)/shard_map/all_to_all | solution.py:34
  27.0 0.0 all-reduce.3.cloned.1.call-start
  27.1 0.0 copy-done.3
  27.1 0.0 copy-done.4
  27.1 1.1 convolution_multiply_fusion.2
  28.2 0.0 copy-done
  28.2 0.0 copy-done.2
  28.2 1.5 fusion.12
  29.7 0.0 all-reduce.3.cloned.1.call-update
  29.7 0.0 reduce-scatter.4.cloned.1.call-start
  29.8 311.6 %all-to-all-done = bf16[32,1792,128]{1,2,0:T(8,128)(2,1)} async-done(((bf16[32,1792,128]{1,2,0:T(8,128)(2,1)}), bf16[32,1792,128]{1,2,0:T(8,128)(2,1)}, u32[]{:S(2)}, u32[]{:S(2)}) %all-to-all-start) | async-done | bytes 14680096 | tf_op jit(solution)/shard_map/all_to_all | solution.py:34
  341.3 13.1 %fusion.11 = f32[512,4096]{1,0:T(8,128)} fusion(bf16[512,1792]{1,0:T(8,128)(2,1)S(1)} %copy-done.2, bf16[1792,4096]{0,1:T(8,128)(2,1)} %bitcast.1), kind=kOutput, calls=%fused_computation.25 | convolution fusion | flops 7516192768 | bytes 24903680 | tf_op jit(solution)/shard_map/dot_general | solution.py:31
  354.4 0.0 reduce-scatter.4.cloned.1.call-update
  354.4 0.0 reduce-scatter.8.cloned.1.call-start
  354.5 0.4 multiply_reduce_fusion
  354.9 16.4 %psum.21 = f32[512]{0:T(512)S(1)} all-reduce(f32[512]{0:T(512)S(1)} %multiply_reduce_fusion), channel_id=1, replica_groups=mesh['dp'=32,'tensor'=8] {'tensor'}, use_global_device_ids=true, to_apply=%region_2.0 | all-reduce | flops 512 | bytes 4096 | tf_op jit(solution)/shard_map/psum | solution.py:23
  371.3 0.0 all-reduce.3.cloned.1.call-done
  371.4 0.0 copy-start.1
  371.4 1.6 multiply_reduce_fusion.1
  373.0 2.6 convolution_multiply_fusion.1
  375.6 0.0 reduce-scatter.8.cloned.1.call-update
  375.6 0.0 reduce-scatter.6.cloned.1.call-start
  375.7 0.0 copy-done.1
  375.7 3.1 fusion.2
  378.8 0.0 reduce-scatter.6.cloned.1.call-update
  378.9 73.3 %reduce-scatter.4.cloned.1.call-done = f32[512,512]{1,0:T(8,128)} async-done(((f32[512,4096]{1,0:T(8,128)}), f32[512,512]{1,0:T(8,128)}) %reduce-scatter.4.cloned.1.call-update) | async-done | bytes 1048592 | tf_op jit(solution)/shard_map/reduce_scatter | solution.py:38
  452.1 2.4 fusion.1
  454.5 117.0 %reduce-scatter.8.cloned.1.call-done = f32[8,512]{1,0:T(8,128)} async-done(((f32[256,512]{1,0:T(8,128)}), f32[8,512]{1,0:T(8,128)}) %reduce-scatter.8.cloned.1.call-update) | async-done | bytes 16400 | tf_op jit(solution)/shard_map/reduce_scatter | solution.py:59
  571.5 121.5 %reduce-scatter.6.cloned.1.call-done = f32[8,1792]{1,0:T(8,128)} async-done(((f32[256,1792]{1,0:T(8,128)}), f32[8,1792]{1,0:T(8,128)}) %reduce-scatter.6.cloned.1.call-update) | async-done | bytes 57360 | tf_op jit(solution)/shard_map/reduce_scatter | solution.py:58
  (5 shorter events, 0.1 us)
Async XLA Ops:
  7.2 21.1 %copy-start = (bf16[256,1792]{1,0:T(8,128)(2,1)S(1)}, bf16[256,1792]{1,0:T(8,128)(2,1)}, u32[]{:S(2)}) copy-start(bf16[256,1792]{1,0:T(8,128)(2,1)} %param.7) | copy-start | bytes 2752516
  15.3 11.8 %copy-start.3 = (bf16[512,512]{1,0:T(8,128)(2,1)S(1)}, bf16[512,512]{1,0:T(8,128)(2,1)}, u32[]{:S(2)}) copy-start(bf16[512,512]{1,0:T(8,128)(2,1)} %param.9) | copy-start | bytes 1572868
  15.3 11.8 %copy-start.4 = (bf16[256,512]{1,0:T(8,128)(2,1)S(1)}, bf16[256,512]{1,0:T(8,128)(2,1)}, u32[]{:S(2)}) copy-start(bf16[256,512]{1,0:T(8,128)(2,1)} %param.8) | copy-start | bytes 786436
  15.3 12.9 %copy-start.2 = (bf16[512,1792]{1,0:T(8,128)(2,1)S(1)}, bf16[512,1792]{1,0:T(8,128)(2,1)}, u32[]{:S(2)}) copy-start(bf16[512,1792]{1,0:T(8,128)(2,1)} %param.5) | copy-start | bytes 5505028
  15.4 326.0 %all-to-all-start = ((bf16[32,1792,128]{1,2,0:T(8,128)(2,1)}), bf16[32,1792,128]{1,2,0:T(8,128)(2,1)}, u32[]{:S(2)}, u32[]{:S(2)}) async-start(bf16[32,1792,128]{1,2,0:T(8,128)(2,1)} %stack.2), calls=%async_computation | async-start | bytes 29360128 | tf_op jit(solution)/shard_map/all_to_all | solution.py:34
  27.0 344.3 %all-reduce.3.cloned.1.call-start = ((), (), s32[]{:S(2)}) async-start(), calls=%async_computation.7 | async-start | bytes 2097152 | tf_op jit(solution)/shard_map/psum | solution.py:23
  29.7 422.4 %reduce-scatter.4.cloned.1.call-start = ((), (), s32[]{:S(2)}) async-start(), calls=%async_computation.4 | async-start | bytes 9437184 | tf_op jit(solution)/shard_map/reduce_scatter | solution.py:38
  354.4 217.1 %reduce-scatter.8.cloned.1.call-start = ((), (), s32[]{:S(2)}) async-start(), calls=%async_computation.6 | async-start | bytes 540672 | tf_op jit(solution)/shard_map/reduce_scatter | solution.py:59
  371.4 4.3 copy-start.1
  375.6 317.4 %reduce-scatter.6.cloned.1.call-start = ((), (), s32[]{:S(2)}) async-start(), calls=%async_computation.5 | async-start | bytes 1892352 | tf_op jit(solution)/shard_map/reduce_scatter | solution.py:58
Sparse Core Ops, SparseCore 0:
  31.1 107.4 all-reduce.2
  354.6 97.5 reduce-scatter.3
  456.7 114.7 reduce-scatter.7
  576.6 116.3 reduce-scatter.5
